TPU v7x, 128 devices: a whole 4x4x4 slice. The times are simulated.
128 devices in a mesh: doc: 8 (over x, core), term: 16 (over z, y).
Axes of the slice: x: 4, y: 4, z: 4, core: 2. Of those that a mesh axis runs over, the one named last changes fastest.
Arguments:
- query_states: bfloat16 [512, 32, 768], P('doc'), may hold values from -6 to 6
- token_ids: int32 [512, 32], P('doc'), may hold values from 0 to 30521, as said below
- transform_weight: bfloat16 [768, 768], replicated, may hold values from -0.21875 to 0.21875
- transform_bias: float32 [768], replicated, may hold values from -3 to 3
- norm_gain: float32 [768], replicated, may hold values from 0.5 to 1.5
- norm_bias: float32 [768], replicated, may hold values from -3 to 3
- decoder_weight: bfloat16 [768, 30720], P(None, 'term'), may hold values from -0.21875 to 0.21875
- decoder_bias: float32 [30720], P('term'), may hold values from -2.5 to 0.5
- candidates: int32 [512, 32], P('doc'), may hold values from 0 to 127, all different within a row; in each aligned block of 64 rows (0 to 63, 64 to 127, ...) at most 32 rows name the same one
- occupancy: int32 [128, 240], P('doc', 'term'), may hold values 0 or 1
- doc_blocks: bfloat16 [128, 240, 128, 128], P('doc', 'term'), may hold values from -0.046875 to 0.046875
Outputs:
- query_weights: bfloat16 [512, 30720], P('doc', 'term')
- scores: float32 [512, 32, 128], P('doc', None, 'term')
Inputs may be any that keep to these rules, and one draw needn't show every extreme that they name: `token_ids`: id 0 marks padding: a query has non-zero ids at its first positions, at least 8 of them, and 0 after them. `candidates`: A query names 32 different tiles; among the 64 queries of one doc index no tile is named by more than 32 of them.
All inputs are finite; a program needn't handle non-finite values. No bound on the sum of `occupancy` on one device may be relied on, other than what follows from the above.
Results may differ from a plain program's by a relative error of at most 0.0041.
Values may be sent and summed in bfloat16 or wider, within the bound.
A program may use at most 128 MiB of HBM per device.

v0:
```python
import jax
import jax.numpy as jnp
from jax import lax
from jax.sharding import PartitionSpec as P

VOCAB = 30522
MOST = 32


def tile_ranks(cand_rows, tile_total):
    tile_index = lax.iota(jnp.int32, tile_total)
    tile_hits = jnp.sum((cand_rows[..., None] == tile_index).astype(jnp.int32), axis=-2)
    tile_before = jnp.cumsum(tile_hits, axis=-2) - tile_hits
    return (tile_hits, tile_before)


def slot_sources(hits_by_tile, before_by_tile, capacity):
    row_total = hits_by_tile.shape[-1]
    slot_index = lax.iota(jnp.int32, capacity)
    chosen = (hits_by_tile[..., None, :] > 0) & (
        before_by_tile[..., None, :] == slot_index[:, None]
    )
    source_row = jnp.sum(jnp.where(chosen, lax.iota(jnp.int32, row_total), 0), axis=-1)
    return (source_row, jnp.any(chosen, axis=-1))


def body(
    query_states,
    token_ids,
    transform_weight,
    transform_bias,
    norm_gain,
    norm_bias,
    decoder_weight,
    decoder_bias,
    candidates,
    occupancy,
    doc_blocks,
):
    query_count, query_length, model_width = query_states.shape
    vocab_local = decoder_weight.shape[1]
    tile_local, blocks_local, tile_docs, block_terms = doc_blocks.shape
    cand_count = candidates.shape[1]
    term_index = lax.axis_index("term")
    doc_index = lax.axis_index("doc")
    doc_count = lax.axis_size("doc")
    term_count = lax.axis_size("term")
    tile_total = doc_count * tile_local
    hidden = (
        jnp.dot(
            query_states.reshape(query_count * query_length, model_width),
            transform_weight,
            preferred_element_type=jnp.float32,
        )
        + transform_bias
    )
    hidden = jax.nn.gelu(hidden, approximate=False)
    centred = hidden - jnp.mean(hidden, axis=-1, keepdims=True)
    spread = jnp.mean(centred * centred, axis=-1, keepdims=True)
    normed = (centred * lax.rsqrt(spread + 1e-06) * norm_gain + norm_bias).astype(jnp.bfloat16)
    logits = jnp.dot(normed, decoder_weight, preferred_element_type=jnp.float32) + decoder_bias
    activated = jnp.log1p(jnp.maximum(logits, 0.0)).reshape(query_count, query_length, vocab_local)
    live_mask = (token_ids != 0).astype(jnp.float32)[:, :, None]
    columns = term_index * vocab_local + lax.iota(jnp.int32, vocab_local)
    vocab_keep = (columns < VOCAB).astype(jnp.float32)
    weights = (jnp.max(activated * live_mask, axis=1) * vocab_keep).astype(jnp.bfloat16)
    own_hits, own_before = tile_ranks(candidates, tile_total)
    all_weights, all_cand = (
        lax.all_gather(weights, "doc", axis=0, tiled=True),
        lax.all_gather(candidates, "doc", axis=0, tiled=True),
    )
    local_cand = (all_cand - doc_index * tile_local).reshape(doc_count, query_count, cand_count)
    tile_hits, tile_before = tile_ranks(local_cand, tile_local)
    source_row, slot_valid = slot_sources(
        jnp.swapaxes(tile_hits, 1, 2), jnp.swapaxes(tile_before, 1, 2), MOST
    )
    flat_index = lax.iota(jnp.int32, doc_count)[:, None, None] * query_count + source_row
    buffer = jnp.take(all_weights, flat_index.reshape(-1), axis=0).reshape(
        doc_count, tile_local, MOST, vocab_local
    )
    buffer = buffer * slot_valid.astype(jnp.bfloat16)[..., None]
    occupied = occupancy.astype(jnp.bfloat16)
    masked = (
        buffer.reshape(doc_count, tile_local, MOST, blocks_local, block_terms)
        * occupied[None, :, None, :, None]
    )
    partial_value = jnp.einsum(
        "jtrbc,tbdc->jtrd", masked, doc_blocks, preferred_element_type=jnp.float32
    )
    slice_width = tile_docs // term_count
    score_total = lax.psum(partial_value, "term")
    score_share = lax.dynamic_slice_in_dim(score_total, term_index * slice_width, slice_width, 3)
    returned = lax.all_to_all(score_share, "doc", split_axis=0, concat_axis=1, tiled=True)
    slot_rank = jnp.take_along_axis(own_before, candidates, axis=1)
    flat_index = candidates * MOST + slot_rank
    scores = jnp.take(returned.reshape(-1, slice_width), flat_index.reshape(-1), axis=0)
    scores = scores.reshape(query_count, cand_count, slice_width)
    return (weights, scores)


def solution(mesh):
    placed = (
        P("doc", None, None),
        P("doc", None),
        P(),
        P(),
        P(),
        P(),
        P(None, "term"),
        P("term"),
        P("doc", None),
        P("doc", "term"),
        P("doc", "term", None, None),
    )
    return jax.shard_map(
        body,
        mesh=mesh,
        in_specs=placed,
        out_specs=(P("doc", "term"), P("doc", None, "term")),
        check_vma=False,
    )
```

profile of v0, /device:TPU:1, one launch (start us, length us, event | category | flops | bytes accessed | tf_op | source)
XLA Modules:
  0.0 286.4 jit_solution(9171432627118115750)
XLA Ops:
  7.2 0.9 copy.49
  8.2 0.9 copy-done
  9.1 17.5 %fusion.25 = (f32[2048]{0:T(1024)S(1)}, f32[2048,768]{0,1:T(8,128)S(1)}) fusion(f32[768]{0:T(1024)} %param.14, bf16[2048,768]{1,0:T(8,128)(2,1)S(1)} %bitcast.34, bf16[768,768]{1,0:T(8,128)(2,1)} %param.13), kind=kOutput, calls=%fused_computation.67 | convolution fusion | flops 2519726080 | bytes 10628096 | tf_op jit(solution)/shard_map/dot_general | solution.py:50
  26.6 0.7 multiply_reduce_fusion.1
  27.4 1.1 copy-done.4
  28.5 13.7 %multiply_reduce_fusion = f32[64,1920]{1,0:T(8,128)S(1)} fusion(f32[64,32]{1,0:T(8,128)S(1)} %compare_convert_fusion, f32[1920]{0:T(1024)S(1)} %copy-done.5, bf16[768,1920]{1,0:T(8,128)(2,1)S(1)} %copy-done.4, f32[2048,768]{0,1:T(8,128)S(1)} %get-tuple-element.7, f32[768]{0:T(1024)S(1)} %copy-done.6, f32[768]{0:T(1024)S(1)} %copy-done.7, ...), kind=kOutput, calls=%fused_computation.6 | convolution fusion | flops 6063267840 | bytes 9770496 | tf_op jit(solution)/shard_map/dot_general | solution.py:61
  42.2 0.7 multiply_convert_fusion
  43.0 14.4 %all-gather = s32[8,64,32]{1,2,0:T(8,128)S(1)} all-gather(s32[1,64,32]{1,2,0:T(8,128)S(1)} %bitcast.39), channel_id=1, replica_groups=mesh['doc'=8,'term'=16] {'doc'}, dimensions={0}, use_global_device_ids=true | all-gather | bytes 73728 | tf_op jit(solution)/shard_map/all_gather | solution.py:70
  57.4 0.3 convert_reduce_fusion
  57.9 6.6 %fusion.23 = s32[8,16,64]{1,0,2:T(8,128)S(1)} fusion(s32[8,64,16]{2,0,1:T(8,128)S(1)} %copy.56), kind=kOutput, calls=%fused_computation.43 | output fusion | flops 524288 | bytes 65536 | tf_op jit(solution)/shard_map/jit(cumsum)/reduce_window_sum | solution.py:13
  64.6 2.2 select_reduce_fusion
  67.1 2.3 fusion.17
  69.4 2.2 all-gather.3.cloned.1.call-done
  71.6 31.8 %gather_fusion = bf16[4096,1920]{1,0:T(8,128)(2,1)} fusion(bf16[512,1920]{1,0:T(8,128)(2,1)} %all-gather.3.cloned.1.call-done, s32[4096]{0:T(1024)S(1)} %broadcast_clamp_fusion), kind=kCustom, calls=%fused_computation | custom fusion | bytes 31473664 | tf_op jit(solution)/shard_map/jit(_take)/gather | solution.py:78
  103.4 27.2 %gather.18 = bf16[8,16,32,15,128]{4,3,2,1,0:T(8,128)(2,1)} reshape(bf16[4096,1920]{1,0:T(8,128)(2,1)} %gather_fusion) | data formatting | bytes 31457280 | tf_op jit(solution)/shard_map/jit(_take)/gather | solution.py:78
  130.6 14.0 %multiply_multiply_fusion = bf16[8,16,32,15,128]{4,3,2,1,0:T(8,128)(2,1)} fusion(bf16[8,16,32,15,128]{4,3,2,1,0:T(8,128)(2,1)} %gather.18, pred[8,16,32]{2,1,0:T(8,128)(4,1)S(1)} %get-tuple-element.4, bf16[16,15]{1,0:T(8,128)(2,1)S(1)} %convert_element_type.39, bf16[8,16,32]{2,1,0:T(8,128)(2,1)S(1)} %convert_element_type.38), kind=kLoop, calls=%fused_computation.3 | loop fusion | flops 23592960 | bytes 31470048 | tf_op jit(solution)/shard_map/mul | solution.py:84
  144.6 13.5 %fusion.18 = f32[8,16,32,128]{3,2,0,1:T(8,128)} fusion(bf16[16,15,128,128]{3,2,1,0:T(8,128)(2,1)} %param.21, bf16[8,16,32,15,128]{4,3,2,1,0:T(8,128)(2,1)} %multiply_multiply_fusion), kind=kOutput, calls=%fused_computation.39 | convolution fusion | flops 2013265920 | bytes 25690112 | tf_op jit(solution)/shard_map/jtrbc,tbdc->jtrd/dot_general | solution.py:87
  158.2 0.4 convert_reduce_fusion.1
  158.8 13.1 %gather_fusion.2 = s32[2048]{0:T(1024)S(1)} fusion(s32[64,128]{1,0:T(8,128)S(1)} %sub.26, s32[2048]{0:T(1024)S(1)} %reshape.174), kind=kCustom, calls=%fused_computation.2 | custom fusion | bytes 32768 | tf_op jit(solution)/shard_map/jit(take_along_axis)/gather | solution.py:94
  172.1 75.3 %all-reduce.2.cloned.1.call-done = f32[8,16,32,128]{3,2,0,1:T(8,128)} async-done(((f32[8,16,32,128]{3,2,0,1:T(8,128)}), f32[8,16,32,128]{3,2,0,1:T(8,128)}) %all-reduce.2.cloned.1.call-update) | async-done | bytes 2097168 | tf_op jit(solution)/shard_map/psum | solution.py:91
  247.4 2.2 constant_dynamic-slice_fusion
  249.6 0.6 copy.60
  250.2 0.9 reshape.192
  251.1 6.0 %all-to-all-start = ((f32[8,1,4096]{2,1,0:T(1,128)}), f32[8,1,4096]{2,1,0:T(1,128)S(1)}, u32[]{:S(2)}, u32[]{:S(2)}) async-start(f32[8,1,4096]{2,1,0:T(1,128)} %reshape.192), calls=%async_computation | async-start | bytes 262144 | tf_op jit(solution)/shard_map/all_to_all | solution.py:93
  257.1 5.3 %all-to-all-done = f32[8,1,4096]{2,1,0:T(1,128)S(1)} async-done(((f32[8,1,4096]{2,1,0:T(1,128)}), f32[8,1,4096]{2,1,0:T(1,128)S(1)}, u32[]{:S(2)}, u32[]{:S(2)}) %all-to-all-start) | async-done | bytes 131104 | tf_op jit(solution)/shard_map/all_to_all | solution.py:93
  262.4 0.5 broadcast.159
  262.9 1.0 reduce
  263.8 1.0 reshape.193
  264.8 3.2 %copy.66 = f32[8,16,32,8]{3,2,1,0:T(8,128)} copy(f32[8,16,32,8]{2,3,1,0:T(8,128)} %bitcast.38) | data formatting | bytes 262144 | tf_op jit(solution)/shard_map/reshape | solution.py:96
  268.0 9.1 %gather_fusion.1 = f32[2048,8]{1,0:T(8,128)} fusion(f32[4096,8]{1,0:T(8,128)} %bitcast.35, s32[2048]{0:T(1024)S(1)} %broadcast_clamp_fusion.1), kind=kCustom, calls=%fused_computation.1 | custom fusion | bytes 139264 | tf_op jit(solution)/shard_map/jit(_take)/gather | solution.py:96
  277.1 1.8 copy.63
  278.9 0.7 broadcast_select_fusion
  (44 shorter events, 1.3 us)
Async XLA Ops:
  7.2 1.9 copy-start
  7.2 64.4 %all-gather.3.cloned.1.call-start = ((), (), s32[]{:S(2)}) async-start(), calls=%async_computation.1 | async-start | bytes 2211840 | tf_op jit(solution)/shard_map/all_gather | solution.py:69
  26.6 1.8 copy-start.4
  26.6 1.8 copy-start.5
  26.6 1.8 copy-start.6
  26.6 1.8 copy-start.7
  28.4 14.5 %copy-start.3 = (s32[16,15]{1,0:T(8,128)S(1)}, s32[16,15]{1,0:T(8,128)}, u32[]{:S(2)}) copy-start(s32[16,15]{1,0:T(8,128)} %param.20) | copy-start | bytes 2884
  28.4 14.6 %copy-start.2 = (s32[64,32]{0,1:T(8,128)S(1)}, s32[64,32]{0,1:T(8,128)}, u32[]{:S(2)}) copy-start(s32[64,32]{0,1:T(8,128)} %param.19) | copy-start | bytes 24580
  42.9 204.5 %all-reduce.2.cloned.1.call-start = ((), (), s32[]{:S(2)}) async-start(), calls=%async_computation.2 | async-start | bytes 4194304 | tf_op jit(solution)/shard_map/psum | solution.py:91
  251.1 11.2 %all-to-all-start = ((f32[8,1,4096]{2,1,0:T(1,128)}), f32[8,1,4096]{2,1,0:T(1,128)S(1)}, u32[]{:S(2)}, u32[]{:S(2)}) async-start(f32[8,1,4096]{2,1,0:T(1,128)} %reshape.192), calls=%async_computation | async-start | bytes 262144 | tf_op jit(solution)/shard_map/all_to_all | solution.py:93
  264.8 14.8 %copy-start.1 = (bf16[64,32,768]{2,1,0:T(8,128)(2,1)S(1)}, bf16[64,32,768]{2,1,0:T(8,128)(2,1)}, u32[]{:S(2)}) copy-start(bf16[64,32,768]{2,1,0:T(8,128)(2,1)} %param.11) | copy-start | bytes 9437188
Sparse Core Ops, SparseCore 0:
  43.0 28.5 all-gather.2
  158.2 89.1 all-reduce.1
where the time goes:
time: 288 us; the launch traced here: 286 us
  local copies, waits for them, and re-layouts  95 us (33%)
  waiting for transfers between devices  82.8 us (29%)
  matrix products  44.7 us (16%)
  other arithmetic  29.1 us (10%)
  blocking collectives  14.4 us (5%)
  between operations  14.3 us (5%)
  starting transfers between devices  6.05 us (2%)
    psum x1, waiting for transfers between devices, body(): score_total = lax.psum(partial_value, 'term')  75.3 us
    gather x2, local copies, waits for them, and re-layouts, body(): jnp.take(all_weights, flat_index.reshape(-1), axis=0)  59 us
    dot_general x1, matrix products, body(): jnp.dot(query_states.reshape(query_count * query_length, model_width), tr...  17.5 us
    all_gather x1, blocking collectives, body(): lax.all_gather(candidates, 'doc', axis=0, tiled=True)  14.4 us
    mul x1, other arithmetic, body(): buffer.reshape(doc_count, tile_local, MOST, blocks_local, block_terms)  14 us
    dot_general x1, matrix products, body(): jnp.dot(normed, decoder_weight, preferred_element_type=jnp.float32)  13.7 us
    dot_general x1, matrix products, body(): jnp.einsum('jtrbc,tbdc->jtrd', masked, doc_blocks, preferred_element_type...  13.5 us
    gather x3, local copies, waits for them, and re-layouts, body(): slot_rank = jnp.take_along_axis(own_before, candidates, axis=1)  13.2 us
  transfers between devices with their start and end apart: 3, of which 3 were waited for; matrix products, arithmetic and copies ran while one was open for 9% of the time, Pallas kernels for 0%

commit v1 on v0

--- a/solution.py
+++ b/solution.py
@@ -88,7 +88,11 @@
         "jtrbc,tbdc->jtrd", masked, doc_blocks, preferred_element_type=jnp.float32
     )
     slice_width = tile_docs // term_count
-    score_total = lax.psum(partial_value, "term")
+    score_total = partial_value
+    for hop in (1, 2, 4, 8):
+        score_total = score_total + lax.ppermute(
+            score_total, "term", [(dev, dev ^ hop) for dev in range(16)]
+        )
     score_share = lax.dynamic_slice_in_dim(score_total, term_index * slice_width, slice_width, 3)
     returned = lax.all_to_all(score_share, "doc", split_axis=0, concat_axis=1, tiled=True)
     slot_rank = jnp.take_along_axis(own_before, candidates, axis=1)

time: 288 us -> 390 us (1.35)
  waiting for transfers between devices: 82.8 us -> 171 us
  starting transfers between devices: 6.05 us -> 15.8 us
  other arithmetic: 29.1 us -> 34.6 us
    ppermute x0 -> x4, waiting for transfers between devices: none -> 163 us  [body(): lax.ppermute(score_total, 'term', [(dev, dev ^ hop) for dev in range(16)])]
    psum x1 -> x0, waiting for transfers between devices: 75.3 us -> none  [body(): score_total = lax.psum(partial_value, 'term')]
    ppermute x0 -> x4, starting transfers between devices: none -> 8.66 us  [body(): lax.ppermute(score_total, 'term', [(dev, dev ^ hop) for dev in range(16)])]
    add x0 -> x4, other arithmetic: none -> 5.53 us  [body(): score_total + lax.ppermute(score_total, 'term', [(dev, dev ^ hop) for dev...]
  transfers between devices with their start and end apart: 3 -> 6, of which waited for: 3 -> 6; matrix products, arithmetic and copies ran while one was open for 9% -> 7% of each run, Pallas kernels for 0% -> 0%
where the time goes in v1:
time: 390 us; the launch traced here: 388 us
  waiting for transfers between devices  171 us (44%)
  local copies, waits for them, and re-layouts  94.4 us (24%)
  matrix products  43.9 us (11%)
  other arithmetic  34.6 us (9%)
  starting transfers between devices  15.8 us (4%)
  blocking collectives  14.4 us (4%)
  between operations  14.3 us (4%)
    ppermute x4, waiting for transfers between devices, body(): lax.ppermute(score_total, 'term', [(dev, dev ^ hop) for dev in range(16)])  163 us
    gather x2, local copies, waits for them, and re-layouts, body(): jnp.take(all_weights, flat_index.reshape(-1), axis=0)  59 us
    dot_general x1, matrix products, body(): jnp.dot(query_states.reshape(query_count * query_length, model_width), tr...  17.5 us
    all_gather x1, blocking collectives, body(): lax.all_gather(candidates, 'doc', axis=0, tiled=True)  14.4 us
    mul x1, other arithmetic, body(): buffer.reshape(doc_count, tile_local, MOST, blocks_local, block_terms)  14 us
    dot_general x1, matrix products, body(): jnp.dot(normed, decoder_weight, preferred_element_type=jnp.float32)  13.7 us
    gather x3, local copies, waits for them, and re-layouts, body(): slot_rank = jnp.take_along_axis(own_before, candidates, axis=1)  13.2 us
    dot_general x1, matrix products, body(): jnp.einsum('jtrbc,tbdc->jtrd', masked, doc_blocks, preferred_element_type...  12.7 us
  transfers between devices with their start and end apart: 6, of which 6 were waited for; matrix products, arithmetic and copies ran while one was open for 7% of the time, Pallas kernels for 0%

profile of v1, /device:TPU:1, one launch (start us, length us, event | category | flops | bytes accessed | tf_op | source)
XLA Modules:
  0.0 388.4 jit_solution(14077223139723578866)
XLA Ops:
  7.2 0.9 copy.49
  9.1 17.5 %fusion.25 = (f32[2048]{0:T(1024)S(1)}, f32[2048,768]{0,1:T(8,128)S(1)}) fusion(f32[768]{0:T(1024)} %param.14, bf16[2048,768]{1,0:T(8,128)(2,1)S(1)} %bitcast.34, bf16[768,768]{1,0:T(8,128)(2,1)} %param.13), kind=kOutput, calls=%fused_computation.67 | convolution fusion | flops 2519726080 | bytes 10628096 | tf_op jit(solution)/shard_map/dot_general | solution.py:50
  27.4 1.1 copy-done.4
  28.5 13.7 %multiply_reduce_fusion = f32[64,1920]{1,0:T(8,128)S(1)} fusion(f32[64,32]{1,0:T(8,128)S(1)} %compare_convert_fusion, f32[1920]{0:T(1024)S(1)} %copy-done.5, bf16[768,1920]{1,0:T(8,128)(2,1)S(1)} %copy-done.4, f32[2048,768]{0,1:T(8,128)S(1)} %get-tuple-element.7, f32[768]{0:T(1024)S(1)} %copy-done.6, f32[768]{0:T(1024)S(1)} %copy-done.7, ...), kind=kOutput, calls=%fused_computation.6 | convolution fusion | flops 6063267840 | bytes 9770496 | tf_op jit(solution)/shard_map/dot_general | solution.py:61
  43.0 14.4 %all-gather = s32[8,64,32]{1,2,0:T(8,128)S(1)} all-gather(s32[1,64,32]{1,2,0:T(8,128)S(1)} %bitcast.39), channel_id=1, replica_groups=mesh['doc'=8,'term'=16] {'doc'}, dimensions={0}, use_global_device_ids=true | all-gather | bytes 73728 | tf_op jit(solution)/shard_map/all_gather | solution.py:70
  57.8 6.6 %fusion.23 = s32[8,16,64]{1,0,2:T(8,128)S(1)} fusion(s32[8,64,16]{2,0,1:T(8,128)S(1)} %copy.56), kind=kOutput, calls=%fused_computation.44 | output fusion | flops 524288 | bytes 65536 | tf_op jit(solution)/shard_map/jit(cumsum)/reduce_window_sum | solution.py:13
  64.6 2.2 select_reduce_fusion
  67.0 2.3 fusion.17
  69.4 2.3 all-gather.3.cloned.1.call-done
  71.6 31.8 %gather_fusion = bf16[4096,1920]{1,0:T(8,128)(2,1)} fusion(bf16[512,1920]{1,0:T(8,128)(2,1)} %all-gather.3.cloned.1.call-done, s32[4096]{0:T(1024)S(1)} %broadcast_clamp_fusion), kind=kCustom, calls=%fused_computation | custom fusion | bytes 31473664 | tf_op jit(solution)/shard_map/jit(_take)/gather | solution.py:78
  103.5 27.2 %gather.18 = bf16[8,16,32,15,128]{4,3,2,1,0:T(8,128)(2,1)} reshape(bf16[4096,1920]{1,0:T(8,128)(2,1)} %gather_fusion) | data formatting | bytes 31457280 | tf_op jit(solution)/shard_map/jit(_take)/gather | solution.py:78
  130.6 14.0 %multiply_multiply_fusion = bf16[8,16,32,15,128]{4,3,2,1,0:T(8,128)(2,1)} fusion(bf16[8,16,32,15,128]{4,3,2,1,0:T(8,128)(2,1)} %gather.18, pred[8,16,32]{2,1,0:T(8,128)(4,1)S(1)} %get-tuple-element.4, bf16[16,15]{1,0:T(8,128)(2,1)S(1)} %convert_element_type.39, bf16[8,16,32]{2,1,0:T(8,128)(2,1)S(1)} %convert_element_type.38), kind=kLoop, calls=%fused_computation.3 | loop fusion | flops 23592960 | bytes 31470048 | tf_op jit(solution)/shard_map/mul | solution.py:84
  144.6 12.7 %fusion.18 = f32[8,16,32,128]{3,2,0,1:T(8,128)S(1)} fusion(bf16[16,15,128,128]{3,2,1,0:T(8,128)(2,1)} %param.21, bf16[8,16,32,15,128]{4,3,2,1,0:T(8,128)(2,1)} %multiply_multiply_fusion), kind=kOutput, calls=%fused_computation.40 | convolution fusion | flops 2013265920 | bytes 25690112 | tf_op jit(solution)/shard_map/jtrbc,tbdc->jtrd/dot_general | solution.py:87
  157.2 1.3 collective-permute-start
  158.5 45.8 %collective-permute-done = f32[8,16,32,128]{3,2,0,1:T(8,128)S(1)} collective-permute-done((f32[8,16,32,128]{3,2,0,1:T(8,128)S(1)}, f32[8,16,32,128]{3,2,0,1:T(8,128)S(1)}, u32[]{:S(2)}, u32[]{:S(2)}) %collective-permute-start) | collective-permute-done | bytes 2097184 | tf_op jit(solution)/shard_map/ppermute | solution.py:93
  204.8 2.8 collective-permute-start.1
  207.6 44.8 %collective-permute-done.1 = f32[8,16,32,128]{3,2,0,1:T(8,128)S(1)} collective-permute-done((f32[8,16,32,128]{3,2,0,1:T(8,128)S(1)}, f32[8,16,32,128]{3,2,0,1:T(8,128)S(1)}, u32[]{:S(2)}, u32[]{:S(2)}) %collective-permute-start.1) | collective-permute-done | bytes 2097184 | tf_op jit(solution)/shard_map/ppermute | solution.py:93
  252.9 1.4 collective-permute-start.2
  254.3 43.9 %collective-permute-done.2 = f32[8,16,32,128]{3,2,0,1:T(8,128)S(1)} collective-permute-done((f32[8,16,32,128]{3,2,0,1:T(8,128)S(1)}, f32[8,16,32,128]{3,2,0,1:T(8,128)S(1)}, u32[]{:S(2)}, u32[]{:S(2)}) %collective-permute-start.2) | collective-permute-done | bytes 2097184 | tf_op jit(solution)/shard_map/ppermute | solution.py:93
  298.7 3.2 collective-permute-start.3
  302.6 13.1 %gather_fusion.2 = s32[2048]{0:T(1024)S(1)} fusion(s32[64,128]{1,0:T(8,128)S(1)} %sub.26, s32[2048]{0:T(1024)S(1)} %reshape.174), kind=kCustom, calls=%fused_computation.2 | custom fusion | bytes 32768 | tf_op jit(solution)/shard_map/jit(take_along_axis)/gather | solution.py:98
  315.9 28.9 %collective-permute-done.3 = f32[8,16,32,128]{3,2,0,1:T(8,128)} collective-permute-done((f32[8,16,32,128]{3,2,0,1:T(8,128)S(1)}, f32[8,16,32,128]{3,2,0,1:T(8,128)}, u32[]{:S(2)}, u32[]{:S(2)}) %collective-permute-start.3) | collective-permute-done | bytes 2097184 | tf_op jit(solution)/shard_map/ppermute | solution.py:93
  344.8 4.0 %dynamic-slice_add_fusion = f32[8,16,32,8]{3,2,0,1:T(8,128)} fusion(f32[8,16,32,128]{3,2,0,1:T(8,128)} %collective-permute-done.3, s32[]{:T(128)S(6)} %select_n.67, f32[8,16,32,128]{3,2,0,1:T(8,128)S(1)} %add.161), kind=kLoop, calls=%fused_computation.33 | loop fusion | flops 32768 | bytes 393220 | tf_op jit(solution)/shard_map/add | solution.py:93
  348.9 2.2 copy.60
  351.1 0.9 reshape.192
  352.0 7.1 %all-to-all-start = ((f32[8,1,4096]{2,1,0:T(1,128)}), f32[8,1,4096]{2,1,0:T(1,128)S(1)}, u32[]{:S(2)}, u32[]{:S(2)}) async-start(f32[8,1,4096]{2,1,0:T(1,128)} %reshape.192), calls=%async_computation | async-start | bytes 262144 | tf_op jit(solution)/shard_map/all_to_all | solution.py:97
  359.1 5.3 %all-to-all-done = f32[8,1,4096]{2,1,0:T(1,128)S(1)} async-done(((f32[8,1,4096]{2,1,0:T(1,128)}), f32[8,1,4096]{2,1,0:T(1,128)S(1)}, u32[]{:S(2)}, u32[]{:S(2)}) %all-to-all-start) | async-done | bytes 131104 | tf_op jit(solution)/shard_map/all_to_all | solution.py:97
  364.9 1.0 reduce
  365.8 1.0 reshape.193
  366.8 3.2 copy.66
  370.0 9.1 %gather_fusion.1 = f32[2048,8]{1,0:T(8,128)} fusion(f32[4096,8]{1,0:T(8,128)} %bitcast.35, s32[2048]{0:T(1024)S(1)} %broadcast_clamp_fusion.1), kind=kCustom, calls=%fused_computation.1 | custom fusion | bytes 139264 | tf_op jit(solution)/shard_map/jit(_take)/gather | solution.py:100
  379.1 1.8 copy.63
  (52 shorter events, 6.8 us)
Async XLA Ops:
  7.2 1.9 copy-start
  7.2 64.4 %all-gather.3.cloned.1.call-start = ((), (), s32[]{:S(2)}) async-start(), calls=%async_computation.1 | async-start | bytes 2211840 | tf_op jit(solution)/shard_map/all_gather | solution.py:69
  26.6 1.8 copy-start.4
  26.6 1.8 copy-start.5
  26.6 1.8 copy-start.6
  26.6 1.8 copy-start.7
  28.4 14.5 %copy-start.3 = (s32[16,15]{1,0:T(8,128)S(1)}, s32[16,15]{1,0:T(8,128)}, u32[]{:S(2)}) copy-start(s32[16,15]{1,0:T(8,128)} %param.20) | copy-start | bytes 2884
  28.4 14.5 %copy-start.2 = (s32[64,32]{0,1:T(8,128)S(1)}, s32[64,32]{0,1:T(8,128)}, u32[]{:S(2)}) copy-start(s32[64,32]{0,1:T(8,128)} %param.19) | copy-start | bytes 24580
  157.2 47.1 %collective-permute-start = (f32[8,16,32,128]{3,2,0,1:T(8,128)S(1)}, f32[8,16,32,128]{3,2,0,1:T(8,128)S(1)}, u32[]{:S(2)}, u32[]{:S(2)}) collective-permute-start(f32[8,16,32,128]{3,2,0,1:T(8,128)S(1)} %fusion.18), channel_id=1, source_target_pairs={{0,1},{1,0},{2,3},{3,2},{4,5},{5,4},{6,7},{7,6},{8,9},{9,8},{10,11... | collective-permute-start | bytes 6291464 | tf_op jit(solution)/shard_map/ppermute | solution.py:93
  204.8 47.6 %collective-permute-start.1 = (f32[8,16,32,128]{3,2,0,1:T(8,128)S(1)}, f32[8,16,32,128]{3,2,0,1:T(8,128)S(1)}, u32[]{:S(2)}, u32[]{:S(2)}) collective-permute-start(f32[8,16,32,128]{3,2,0,1:T(8,128)S(1)} %add.159), channel_id=1, source_target_pairs={{0,2},{1,3},{2,0},{3,1},{4,6},{5,7},{6,4},{7,5},{8,10},{9,11},{10,... | collective-permute-start | bytes 6291464 | tf_op jit(solution)/shard_map/ppermute | solution.py:93
  252.9 45.2 %collective-permute-start.2 = (f32[8,16,32,128]{3,2,0,1:T(8,128)S(1)}, f32[8,16,32,128]{3,2,0,1:T(8,128)S(1)}, u32[]{:S(2)}, u32[]{:S(2)}) collective-permute-start(f32[8,16,32,128]{3,2,0,1:T(8,128)S(1)} %add.160), channel_id=1, source_target_pairs={{0,4},{1,5},{2,6},{3,7},{4,0},{5,1},{6,2},{7,3},{8,12},{9,13},{10,... | collective-permute-start | bytes 6291464 | tf_op jit(solution)/shard_map/ppermute | solution.py:93
  298.7 46.2 %collective-permute-start.3 = (f32[8,16,32,128]{3,2,0,1:T(8,128)S(1)}, f32[8,16,32,128]{3,2,0,1:T(8,128)}, u32[]{:S(2)}, u32[]{:S(2)}) collective-permute-start(f32[8,16,32,128]{3,2,0,1:T(8,128)S(1)} %add.161), channel_id=1, source_target_pairs={{0,8},{1,9},{2,10},{3,11},{4,12},{5,13},{6,14},{7,15},{8,0},{9,1},... | collective-permute-start | bytes 6291464 | tf_op jit(solution)/shard_map/ppermute | solution.py:93
  352.0 12.4 %all-to-all-start = ((f32[8,1,4096]{2,1,0:T(1,128)}), f32[8,1,4096]{2,1,0:T(1,128)S(1)}, u32[]{:S(2)}, u32[]{:S(2)}) async-start(f32[8,1,4096]{2,1,0:T(1,128)} %reshape.192), calls=%async_computation | async-start | bytes 262144 | tf_op jit(solution)/shard_map/all_to_all | solution.py:97
  366.8 14.8 %copy-start.1 = (bf16[64,32,768]{2,1,0:T(8,128)(2,1)S(1)}, bf16[64,32,768]{2,1,0:T(8,128)(2,1)}, u32[]{:S(2)}) copy-start(bf16[64,32,768]{2,1,0:T(8,128)(2,1)} %param.11) | copy-start | bytes 9437188
Sparse Core Ops, SparseCore 0:
  43.0 28.5 all-gather.2
